TPU v7x, 32 devices: a whole 2x2x4 slice. The times are simulated.
32 devices in a mesh: pole: 2 (over core), row: 4 (over y, x), col: 4 (over z).
Axes of the slice: x: 2, y: 2, z: 4, core: 2. Of those that a mesh axis runs over, the one named last changes fastest.
Arguments:
- inverse_trail: bfloat16 [2, 1024, 2, 1024], P('pole', 'row', None, 'col'), may hold values from -6 to 6
- lower_t: bfloat16 [2, 2048, 2, 1024], P('pole', 'col', None, 'row'), may hold values from -0.125 to 0.125
- diag_inverse: bfloat16 [2, 2048, 2, 2048], P('pole', 'row', None, 'col'), may hold values from -6 to 6
- pole_weight: float32 [256, 2], replicated, may hold values from -4 to 4
- pole_slot: int32 [2], P('pole'), may hold values from 0 to 255
- pair_row: int32 [1024], replicated, may hold values from 0 to 383, as said below
- pair_col: int32 [1024], replicated, may hold values from 0 to 255, as said below
- projector: bfloat16 [1024, 64], P('pole'), may hold values from -6 to 6
Outputs:
- diag_block: bfloat16 [2, 2048, 2, 2048], P('pole', 'row', None, 'col')
- pair_density: float32 [1024, 128], P('pole')
Inputs may be any that keep to these rules, and one draw needn't show every extreme that they name: `pair_row`: pairs come in aligned blocks of 512, one block for each index of pole. A pair's grid cell is (a // (256 // size of row), b // (256 // size of col)) for a supernode row atom a and column atom b, and (b // (256 // size of row), (a - 256) // (128 // size of col)) otherwise. In every block at most 64 pairs share one grid cell, and some cell holds exactly 64. `pair_col`: drawn together with pair_row.
All inputs are finite; a program needn't handle non-finite values.
Results may differ from a plain program's by a relative error of at most 0.0038.
Values may be sent and summed in bfloat16 or wider, within the bound.
A program may use at most 64 MiB of HBM per device.

v0:
```python
import jax
import jax.numpy as jnp
from jax import lax
from jax.sharding import PartitionSpec as P

K = 2048
M = 1024
B = 8
KA = 256


def local(
    inverse_trail, lower_t, diag_inverse, pole_weight, pole_slot, pair_row, pair_col, projector
):
    trail = inverse_trail[0]
    lower = lower_t[0]
    inverse = diag_inverse[0]
    trail_rows = trail.shape[0]
    trail_cols = trail.shape[2]
    upper_half = trail.reshape(trail_rows, 2 * trail_cols)
    lower_half = jnp.concatenate([-trail[:, 1, :], trail[:, 0, :]], axis=1)
    trail_real = jnp.concatenate([upper_half, lower_half], axis=0)
    gathered = lax.all_gather(lower, "col", axis=0, tiled=True)
    flat_lower = gathered.reshape(gathered.shape[0], 2 * trail_rows)
    local_super = K // lax.axis_size("row")
    chosen = flat_lower
    coupling = lax.psum_scatter(
        -jnp.dot(chosen, trail_real, preferred_element_type=jnp.float32),
        "row",
        scatter_dimension=0,
        tiled=True,
    )
    coupling = coupling.astype(jnp.bfloat16).reshape(local_super, 2, trail_cols)
    coupling_all = lax.all_gather(coupling, "col", axis=2, tiled=True)
    lower_all = lax.all_gather(lower, "row", axis=2, tiled=True)
    real_side = jnp.concatenate([lower_all[:, 0, :], -lower_all[:, 1, :]], axis=1)
    imag_side = jnp.concatenate([lower_all[:, 1, :], lower_all[:, 0, :]], axis=1)
    stacked = jnp.concatenate([real_side, imag_side], axis=0)
    coupling_flat = coupling_all.reshape(local_super, 2 * M)
    product = lax.dot_general(
        coupling_flat, stacked, (((1,), (1,)), ((), ())), preferred_element_type=jnp.float32
    )
    super_cols = lower.shape[0]
    product = product.reshape(local_super, 2, super_cols)
    block = (inverse.astype(jnp.float32) - product).astype(jnp.bfloat16)
    row_atoms = local_super // B
    col_atoms = super_cols // B
    trail_atoms = trail_cols // B
    table_super = (
        block.reshape(row_atoms, B, 2, col_atoms, B)
        .transpose(0, 3, 2, 1, 4)
        .reshape(row_atoms * col_atoms, 2 * B * B)
    )
    table_trail = (
        coupling.reshape(row_atoms, B, 2, trail_atoms, B)
        .transpose(3, 0, 2, 4, 1)
        .reshape(trail_atoms * row_atoms, 2 * B * B)
    )
    my_row = lax.axis_index("row")
    my_col = lax.axis_index("col")
    in_super = pair_row < KA
    super_here = in_super & (pair_row // row_atoms == my_row) & (pair_col // col_atoms == my_col)
    super_index = jnp.clip(
        (pair_row - my_row * row_atoms) * col_atoms + pair_col - my_col * col_atoms,
        0,
        row_atoms * col_atoms - 1,
    )
    trail_atom = pair_row - KA
    trail_here = (
        jnp.logical_not(in_super)
        & (pair_col // row_atoms == my_row)
        & (trail_atom // trail_atoms == my_col)
    )
    trail_index = jnp.clip(
        (trail_atom - my_col * trail_atoms) * row_atoms + pair_col - my_row * row_atoms,
        0,
        trail_atoms * row_atoms - 1,
    )
    from_super = jnp.take(table_super, super_index, axis=0).astype(jnp.float32)
    from_trail = jnp.take(table_trail, trail_index, axis=0).astype(jnp.float32)
    chosen = jnp.where(super_here[:, None], from_super, 0.0) + jnp.where(
        trail_here[:, None], from_trail, 0.0
    )
    pair_total = chosen.shape[0]
    chosen = chosen.reshape(pair_total, 2, B * B)
    weight_slot = pole_slot[0]
    selector = (jnp.arange(pole_weight.shape[0], dtype=jnp.int32) == weight_slot).astype(
        jnp.float32
    )
    weight = jnp.sum(selector[:, None] * pole_weight, axis=0)
    real_part = weight[0] * chosen[:, 0] - weight[1] * chosen[:, 1]
    imag_part = weight[0] * chosen[:, 1] + weight[1] * chosen[:, 0]
    pair_term = jnp.stack([real_part, imag_part], axis=1).reshape(pair_total, 2 * B * B)
    grid_width = lax.axis_size("col")
    cells = lax.axis_size("row") * grid_width
    owners = lax.axis_size("pole")
    per_owner = pair_total // owners
    most = 2 * per_owner // cells
    cell_row = jnp.where(in_super, pair_row // row_atoms, pair_col // row_atoms)
    cell_col = jnp.where(in_super, pair_col // col_atoms, jnp.maximum(trail_atom, 0) // trail_atoms)
    cell_id = (cell_row * grid_width + cell_col).reshape(owners, per_owner)
    marks = (cell_id[:, :, None] == jnp.arange(cells, dtype=jnp.int32)[None, None, :]).astype(
        jnp.int32
    )
    ranks = jnp.cumsum(marks, axis=1) - 1
    rank = jnp.take_along_axis(ranks, cell_id[:, :, None], axis=2)[:, :, 0]
    held = (cell_id == my_row * grid_width + my_col).reshape(pair_total)
    target = (jnp.arange(owners, dtype=jnp.int32)[:, None] * most + rank).reshape(pair_total)
    target = jnp.where(held, target, owners * most)
    buffer = (
        jnp.zeros((owners * most, 2 * B * B), jnp.float32).at[target].add(pair_term, mode="drop")
    )
    buffer = buffer.reshape(owners, most, 2 * B * B)
    pooled = lax.psum_scatter(buffer, "pole", scatter_dimension=0, tiled=True).reshape(
        most, 2 * B * B
    )
    collected = lax.all_gather(pooled, ("row", "col"), axis=0, tiled=True)
    my_owner = lax.axis_index("pole")
    own_cell = lax.dynamic_index_in_dim(cell_id, my_owner, 0, keepdims=False)
    own_rank = lax.dynamic_index_in_dim(rank, my_owner, 0, keepdims=False)
    at_owner = jnp.take(collected, own_cell * most + own_rank, axis=0)
    owner_pairs = at_owner.shape[0]
    density = at_owner.reshape(owner_pairs, 2, B * B) * projector.astype(jnp.float32)[:, None, :]
    return (block[None], density.reshape(owner_pairs, 2 * B * B))


def solution(mesh):
    in_specs = (
        P("pole", "row", None, "col"),
        P("pole", "col", None, "row"),
        P("pole", "row", None, "col"),
        P(),
        P("pole"),
        P(),
        P(),
        P("pole", None),
    )
    out_specs = (P("pole", "row", None, "col"), P("pole", None))
    return jax.shard_map(local, mesh=mesh, in_specs=in_specs, out_specs=out_specs, check_vma=False)
```

profile of v0, /device:TPU:0, one launch (start us, length us, event | category | flops | bytes accessed | tf_op | source)
XLA Modules:
  0.0 318.5 jit_solution(15085540868859104944)
XLA Ops:
  7.2 0.0 all-gather.9.cloned.1.call-start
  7.2 0.7 all-gather.9.cloned.1.call-update
  7.9 0.0 reduce-scatter.3.cloned.1.call-start
  7.9 1.0 copy.72
  8.9 1.0 copy.65
  9.9 48.0 %all-gather.9.cloned.1.call-done = bf16[1,2048,2,256]{3,2,0,1:T(2,128)(2,1)} async-done(((bf16[1,512,2,256]{3,2,0,1:T(2,128)(2,1)}), bf16[1,2048,2,256]{3,2,0,1:T(2,128)(2,1)}) %all-gather.9.cloned.1.call-update) | async-done | bytes 2097168 | tf_op jit(solution)/shard_map/all_gather | solution.py:23
  58.0 2.0 copy.66
  60.0 0.0 copy-start.1
  60.0 3.2 %negate_bitcast_fusion = f32[2048,512]{0,1:T(8,128)} fusion(bf16[2048,512]{1,0:T(8,128)(2,1)S(1)} %bitcast.89, bf16[256,256]{1,0:T(8,128)(2,1)S(1)} %get-tuple-element.18, bf16[256,256]{1,0:T(8,128)(2,1)S(1)} %get-tuple-element.17, bf16[256,512]{1,0:T(8,128)(2,1)S(1)} %bitcast.103), kind=kOutput, calls=%fused_computation.6 | convolution fusion | flops 1076363264 | bytes 6815744 | tf_op jit(solution)/shard_map/dot_general | solution.py:28
  63.3 0.0 reduce-scatter.3.cloned.1.call-update
  63.3 0.0 all-gather.11.cloned.1.call-start
  63.3 0.0 copy-done.1
  63.3 0.9 copy.51
  64.2 0.0 all-gather.11.cloned.1.call-update
  64.2 0.0 all-gather.7.cloned.1.call-start
  64.3 0.0 copy-done.3
  64.3 0.0 copy-done.4
  65.0 49.8 %reduce-scatter.3.cloned.1.call-done = f32[512,512]{0,1:T(8,128)} async-done(((f32[2048,512]{0,1:T(8,128)}), f32[512,512]{0,1:T(8,128)}) %reduce-scatter.3.cloned.1.call-update) | async-done | bytes 1048592 | tf_op jit(solution)/shard_map/reduce_scatter | solution.py:27
  114.8 2.1 convert_element_type.37
  116.9 0.0 all-gather.7.cloned.1.call-update
  116.9 0.2 reduce-scatter.5.cloned.1.call-start
  117.2 0.1 broadcast_bitcast_fusion
  117.3 2.3 reduce-window.6
  119.6 0.3 slice_reduce_fusion
  120.0 0.1 bitcast_bitcast_fusion
  120.1 10.5 %gather_fusion.3 = s32[1024]{0:T(1024)S(1)} fusion(s32[2,512,16]{1,2,0:T(8,128)S(1)} %bitcast_bitcast_fusion, s32[1024]{0:T(1024)S(1)} %bitcast.85), kind=kCustom, calls=%fused_computation.3 | custom fusion | bytes 20480 | tf_op jit(solution)/shard_map/jit(take_along_axis)/gather | solution.py:106
  130.7 0.0 copy-done.5
  130.7 0.1 multiply_reduce_fusion
  130.8 0.6 fusion.28
  131.4 20.4 %all-gather.11.cloned.1.call-done = bf16[1,512,2,1024]{3,1,2,0:T(8,128)(2,1)} async-done(((bf16[1,512,2,256]{3,1,2,0:T(8,128)(2,1)}), bf16[1,512,2,1024]{3,1,2,0:T(8,128)(2,1)}) %all-gather.11.cloned.1.call-update) | async-done | bytes 2097168 | tf_op jit(solution)/shard_map/all_gather | solution.py:35
  151.8 1.3 fusion.27
  153.1 1.7 slice_bitcast_fusion
  154.8 0.0 copy-start
  154.8 19.0 %maximum_maximum_fusion = bf16[1024,2048]{1,0:T(8,128)(2,1)} fusion(bf16[512,1024]{1,0:T(8,128)(2,1)S(1)} %get-tuple-element.14, bf16[512,1024]{1,0:T(8,128)(2,1)S(1)} %get-tuple-element.13, bf16[512,1024]{1,0:T(8,128)(2,1)S(1)} %fusion.27), kind=kLoop, calls=%fused_computation.5 | loop fusion | flops 16777216 | bytes 7340032 | tf_op jit(solution)/shard_map/concatenate | solution.py:38
  173.8 0.0 copy-done
  173.8 0.2 copy.56
  174.0 10.9 %reshape_reshape.3 = bf16[64,8,2,32,8]{4,3,2,1,0:T(8,128)(2,1)} reshape(bf16[512,512]{1,0:T(8,128)(2,1)S(1)} %copy.56) | data formatting | bytes 1048576 | tf_op jit(solution)/shard_map/reshape;reshape | solution.py:55
  184.9 11.5 %copy.57 = bf16[32,64,2,8,8]{1,0,4,3,2:T(8,128)(2,1)S(1)} copy(bf16[32,64,2,8,8]{3,0,2,4,1:T(8,128)(2,1)} %bitcast.87) | data formatting | bytes 1048576 | tf_op jit(solution)/shard_map/transpose | solution.py:56
  196.4 0.0 copy-start.6
  196.4 0.8 reshape.285
  197.2 0.3 copy.58
  197.5 3.2 %gather_fusion.1 = bf16[1024,128]{1,0:T(8,128)(2,1)S(1)} fusion(bf16[2048,128]{1,0:T(8,128)(2,1)S(1)} %copy.58, s32[1024]{0:T(1024)S(1)} %get-tuple-element.25), kind=kCustom, calls=%fused_computation.1 | custom fusion | bytes 528384 | tf_op jit(solution)/shard_map/jit(_take)/gather | solution.py:80
  200.7 0.1 copy.59
  200.9 0.0 all-gather.7.cloned.1.call-done
  200.9 0.0 copy-done.6
  200.9 5.2 %fusion = bf16[512,2,512]{2,0,1:T(8,128)(2,1)S(1)} fusion(bf16[512,2048,1]{0,1,2:T(8,128)(2,1)} %bitcast.110, bf16[2,512,2048]{2,1,0:T(8,128)(2,1)} %bitcast.93, bf16[1,512,2,512]{3,2,1,0:T(2,128)(2,1)S(1)} %copy-done.6), kind=kOutput, calls=%fused_computation.8 | convolution fusion | flops 2149056512 | bytes 8388608 | tf_op jit(solution)/shard_map/dot_general | solution.py:40
  206.1 20.6 %reshape.283 = bf16[64,8,2,64,8]{4,3,1,0,2:T(8,128)(2,1)} reshape(bf16[512,2,512]{2,0,1:T(8,128)(2,1)S(1)} %fusion) | data formatting | bytes 2097152 | tf_op jit(solution)/shard_map/reshape | solution.py:50
  226.8 14.0 %copy.53 = bf16[64,64,2,8,8]{1,0,4,3,2:T(8,128)(2,1)S(1)} copy(bf16[64,64,2,8,8]{4,1,3,0,2:T(8,128)(2,1)} %bitcast.86) | data formatting | bytes 2097152 | tf_op jit(solution)/shard_map/transpose | solution.py:51
  240.8 2.5 reshape.284
  243.3 1.6 copy.54
  244.9 3.2 %gather_fusion = bf16[1024,128]{1,0:T(8,128)(2,1)S(1)} fusion(bf16[4096,128]{1,0:T(8,128)(2,1)S(1)} %copy.54, s32[1024]{0:T(1024)S(1)} %get-tuple-element.23), kind=kCustom, calls=%fused_computation | custom fusion | bytes 528384 | tf_op jit(solution)/shard_map/jit(_take)/gather | solution.py:79
  248.1 0.1 copy.55
  248.3 0.1 select_add_fusion
  248.4 1.3 multiply_subtract_fusion
  249.7 0.2 copy.60
  249.9 6.6 %scatter_custom_fusion = f32[128,128]{1,0:T(8,128)} fusion(s32[1024]{0:T(1024)S(1)} %compare_select_fusion.5, f32[1024,128]{1,0:T(8,128)S(1)} %copy.60, f32[]{:T(128)} %constant.147.clone.1), kind=kCustom, calls=%fused_computation.30 | custom fusion | flops 131072 | bytes 65540 | tf_op jit(solution)/shard_map/scatter-add | solution.py:111
  256.5 0.0 reduce-scatter.5.cloned.1.call-update
  256.6 0.0 copy-done.2
  256.6 0.1 copy.61
  256.8 2.0 copy.62
  258.8 5.4 %reduce-scatter.5.cloned.1.call-done = f32[1,64,128]{2,1,0:T(8,128)} async-done(((f32[2,64,128]{2,1,0:T(8,128)}), f32[1,64,128]{2,1,0:T(8,128)}) %reduce-scatter.5.cloned.1.call-update) | async-done | bytes 32784 | tf_op jit(solution)/shard_map/reduce_scatter | solution.py:114
  264.3 45.8 %all-gather.2 = f32[1,1024,128]{2,1,0:T(8,128)S(1)} all-gather(f32[1,64,128]{2,1,0:T(8,128)} %reduce-scatter.5.cloned.1.call-done), channel_id=4, replica_groups=mesh['pole'=2,'row'=4,'col'=4] {'row','col'}, dimensions={1}, use_global_device_ids=true | all-gather | bytes 557056 | tf_op jit(solution)/shard_map/all_gather | solution.py:117
  310.1 1.0 gather_fusion.2
  311.1 0.8 select_multiply_fusion
  (29 shorter events, 0.3 us)
Async XLA Ops:
  7.2 50.8 %all-gather.9.cloned.1.call-start = ((), (), s32[]{:S(2)}) async-start(), calls=%async_computation.5 | async-start | bytes 2621440 | tf_op jit(solution)/shard_map/all_gather | solution.py:23
  7.9 106.9 %reduce-scatter.3.cloned.1.call-start = ((), (), s32[]{:S(2)}) async-start(), calls=%async_computation.2 | async-start | bytes 5242880 | tf_op jit(solution)/shard_map/reduce_scatter | solution.py:27
  60.0 3.3 %copy-start.1 = (bf16[1,512,2,256]{3,2,1,0:T(2,128)(2,1)S(1)}, bf16[1,512,2,256]{3,2,1,0:T(2,128)(2,1)}, u32[]{:S(2)}) copy-start(bf16[1,512,2,256]{3,2,1,0:T(2,128)(2,1)} %param.9) | copy-start | bytes 1572868
  63.3 1.0 copy-start.3
  63.3 1.0 copy-start.4
  63.3 88.5 %all-gather.11.cloned.1.call-start = ((), (), s32[]{:S(2)}) async-start(), calls=%async_computation.6 | async-start | bytes 2621440 | tf_op jit(solution)/shard_map/all_gather | solution.py:35
  64.2 66.5 %copy-start.5 = (f32[256,2]{0,1:T(2,128)S(1)}, f32[256,2]{0,1:T(2,128)}, u32[]{:S(2)}) copy-start(f32[256,2]{0,1:T(2,128)} %param.11) | copy-start | bytes 6148
  64.2 136.7 %all-gather.7.cloned.1.call-start = ((), (), s32[]{:S(2)}) async-start(), calls=%async_computation.3 | async-start | bytes 2621440 | tf_op jit(solution)/shard_map/all_gather | solution.py:34
  116.9 147.3 %reduce-scatter.5.cloned.1.call-start = ((), (), s32[]{:S(2)}) async-start(), calls=%async_computation.4 | async-start | bytes 98304 | tf_op jit(solution)/shard_map/reduce_scatter | solution.py:114
  154.8 19.0 %copy-start = (bf16[512,512]{0,1:T(8,128)(2,1)S(1)}, bf16[512,512]{0,1:T(8,128)(2,1)}, u32[]{:S(2)}) copy-start(bf16[512,512]{0,1:T(8,128)(2,1)} %convert_element_type.37) | copy-start | bytes 1572868
  196.4 4.5 %copy-start.6 = (bf16[1,512,2,512]{3,2,1,0:T(2,128)(2,1)S(1)}, bf16[1,512,2,512]{3,2,1,0:T(2,128)(2,1)}, u32[]{:S(2)}) copy-start(bf16[1,512,2,512]{3,2,1,0:T(2,128)(2,1)} %param.10) | copy-start | bytes 3145732
  243.3 13.3 %copy-start.2 = (bf16[512,64]{0,1:T(8,128)(2,1)S(1)}, bf16[512,64]{0,1:T(8,128)(2,1)}, u32[]{:S(2)}) copy-start(bf16[512,64]{0,1:T(8,128)(2,1)} %param.15) | copy-start | bytes 196612
Sparse Core Ops, SparseCore 0:
  9.5 48.3 all-gather.8
  63.4 51.3 reduce-scatter.2
  116.7 35.0 all-gather.10
  153.8 45.6 all-gather.6
  256.7 7.5 reduce-scatter.4
where the time goes:
time: 319 us; the launch traced here: 318 us
  waiting for transfers between devices  124 us (39%)
  local copies, waits for them, and re-layouts  90.7 us (28%)
  blocking collectives  45.8 us (14%)
  other arithmetic  33.9 us (11%)
  between operations  14.8 us (5%)
  matrix products  8.45 us (3%)
    reduce_scatter x1, waiting for transfers between devices, local(): lax.psum_scatter(-jnp.dot(chosen, trail_real, preferred_element_type=jnp....  49.8 us
    all_gather x1, waiting for transfers between devices, local(): gathered = lax.all_gather(lower, 'col', axis=0, tiled=True)  48 us
    all_gather x1, blocking collectives, local(): collected = lax.all_gather(pooled, ('row', 'col'), axis=0, tiled=True)  45.8 us
    reshape x1, local copies, waits for them, and re-layouts, local(): block.reshape(row_atoms, B, 2, col_atoms, B).transpose(0, 3, 2, 1, 4)  20.6 us
    all_gather x1, waiting for transfers between devices, local(): lower_all = lax.all_gather(lower, 'row', axis=2, tiled=True)  20.4 us
    concatenate x1, other arithmetic, local(): stacked = jnp.concatenate([real_side, imag_side], axis=0)  19 us
    transpose x1, local copies, waits for them, and re-layouts, local(): table_super = block.reshape(row_atoms, B, 2, col_atoms, B).transpose(0, 3...  14 us
    transpose x1, local copies, waits for them, and re-layouts, local(): table_trail = coupling.reshape(row_atoms, B, 2, trail_atoms, B).transpose...  11.5 us
  transfers between devices with their start and end apart: 5, of which 4 were waited for; matrix products, arithmetic and copies ran while one was open for 22% of the time, Pallas kernels for 0%

commit v1 on v0

v1 whole, which is shorter than its diff:
```python
import functools

import jax
import jax.numpy as jnp
from jax import lax
from jax.experimental import pallas as pl
from jax.experimental.pallas import tpu as pltpu
from jax.sharding import PartitionSpec as P

B = 8
HALVES = 2
MESH = pl.DeviceIdType.MESH


def main_kernel(
    n, l_ref, t_ref, inv_ref, idx_ref, weight_ref, proj_ref, block_ref, dens_ref,
    term, pool, coll, slots, term_send, term_recv, coll_send, coll_recv, prod_ref,
    lz, lx, part, own, rs, cz, treal,
    lz_send, lz_recv, lx_send, lx_recv, rs_send, rs_recv, cz_send, cz_recv,
):
    r = lax.axis_index("row")
    c = lax.axis_index("col")
    size = l_ref.shape[0]
    half = size // HALVES
    step = min(128, half)
    width = t_ref.shape[0]
    bf16 = jnp.bfloat16
    f32 = jnp.float32

    barrier = pltpu.get_barrier_semaphore()
    me = lax.axis_index("pole")
    owners = lax.axis_size("pole")
    cells = n * n
    cell = r * n + c

    def peer(j):
        other = lax.rem(cell + j, cells)
        return {"row": other // n, "col": lax.rem(other, n)}, other

    for j in range(1, cells):
        pl.semaphore_signal(barrier, inc=1, device_id=peer(j)[0], device_id_type=MESH)
    for j in range(1, owners):
        pl.semaphore_signal(barrier, inc=1, device_id={"pole": lax.rem(me + j, owners)}, device_id_type=MESH)
    pl.semaphore_wait(barrier, cells - 1 + owners - 1)

    def rows(h):
        return pl.ds(h * half, half)

    def line_copy(src, dst, send, recv, k, h, side):
        to = jnp.maximum(c - 1, 0) if side == 0 else jnp.minimum(c + 1, n - 1)
        return pltpu.make_async_remote_copy(
            src_ref=src,
            dst_ref=dst.at[k, rows(h)],
            send_sem=send.at[side, k, h],
            recv_sem=recv.at[k, h],
            device_id={"col": to},
            device_id_type=MESH,
        )

    def can(side):
        return c > 0 if side == 0 else c < n - 1

    def from_side(side, s):
        k = c + s if side == 0 else c - s
        there = k < n if side == 0 else k >= 0
        return jnp.clip(k, 0, n - 1), there

    def l_copy(k, h, side, mine):
        src = l_ref.at[rows(h)] if mine else lz.at[k, rows(h)]
        return line_copy(src, lz, lz_send, lz_recv, k, h, side)

    def c_copy(k, h, side):
        return line_copy(cz.at[k, rows(h)], cz, cz_send, cz_recv, k, h, side)

    def lx_copy(j):
        return pltpu.make_async_remote_copy(
            src_ref=l_ref,
            dst_ref=lx.at[r],
            send_sem=lx_send.at[j],
            recv_sem=lx_recv.at[r],
            device_id={"row": lax.rem(r + j, n)},
            device_id_type=MESH,
        )

    def lx_wait(j):
        k = lax.rem(r + j, n)
        pltpu.make_async_remote_copy(
            src_ref=l_ref, dst_ref=lx.at[k], send_sem=lx_send.at[j], recv_sem=lx_recv.at[k],
            device_id={"row": k}, device_id_type=MESH,
        ).wait_recv()

    def rs_copy(k, h):
        return pltpu.make_async_remote_copy(
            src_ref=part.at[k, rows(h)],
            dst_ref=rs.at[r, rows(h)],
            send_sem=rs_send.at[k, h],
            recv_sem=rs_recv.at[r, h],
            device_id={"row": k},
            device_id_type=MESH,
        )

    def rs_wait(j, h):
        k = lax.rem(r + j, n)
        pltpu.make_async_remote_copy(
            src_ref=part.at[k, rows(h)], dst_ref=rs.at[k, rows(h)], send_sem=rs_send.at[k, h],
            recv_sem=rs_recv.at[k, h], device_id={"row": k}, device_id_type=MESH,
        ).wait_recv()

    def partial(k, h, mine):
        def one(i, carry):
            at = pl.ds(pl.multiple_of(h * half + i * step, step), step)
            left = l_ref[at] if mine else lz[k, at]
            value = -jnp.dot(left, treal[...], preferred_element_type=f32)

            @pl.when(k == r)
            def _():
                own[at] = value

            @pl.when(k != r)
            def _():
                part[k, at] = value.astype(bf16)

            return carry

        lax.fori_loop(0, half // step, one, 0)

        @pl.when(k != r)
        def _():
            rs_copy(k, h).start()

    def finish():
        for h in range(HALVES):
            for j in range(1, n):
                rs_wait(j, h)

            def one(i, carry):
                at = pl.ds(pl.multiple_of(h * half + i * step, step), step)
                total = own[at]
                for j in range(1, n):
                    total = total + rs[lax.rem(r + j, n), at].astype(f32)
                value = total.astype(bf16)
                cz[c, at] = value
                return carry

            lax.fori_loop(0, half // step, one, 0)
            for side in range(2):
                @pl.when(can(side))
                def _():
                    c_copy(c, h, side).start()

    def accumulate(k, first):
        def with_right(right):
            real = right[:, :width]
            imag = right[:, width:]
            right_re = jnp.concatenate([real, -imag], axis=1)
            right_im = jnp.concatenate([imag, real], axis=1)

            def one(i, carry):
                at = pl.ds(pl.multiple_of(i * step, step), step)
                left = cz[k, at]
                dims = (((1,), (1,)), ((), ()))
                re = lax.dot_general(left, right_re, dims, preferred_element_type=f32)
                im = lax.dot_general(left, right_im, dims, preferred_element_type=f32)
                if first:
                    prod_ref[at, :size] = re
                    prod_ref[at, size:] = im
                else:
                    prod_ref[at, :size] += re
                    prod_ref[at, size:] += im
                return carry

            lax.fori_loop(0, size // step, one, 0)

        @pl.when(k == r)
        def _():
            with_right(l_ref[...])

        @pl.when(k != r)
        def _():
            with_right(lx[k])

    for h in range(HALVES):
        for side in range(2):
            @pl.when(can(side))
            def _():
                l_copy(c, h, side, True).start()

    trail_re = t_ref[:, :width]
    trail_im = t_ref[:, width:]
    treal[:width, :width] = trail_re
    treal[:width, width:] = trail_im
    treal[width:, :width] = -trail_im
    treal[width:, width:] = trail_re
    for h in range(HALVES):
        partial(c, h, True)
    lx_copy(1).start()

    per_owner = idx_ref.shape[2]
    most = 2 * per_owner // cells
    held_rows = most * B
    chunk = min(128, held_rows)
    earlier = (
        lax.broadcasted_iota(jnp.int32, (per_owner, per_owner), 0)
        < lax.broadcasted_iota(jnp.int32, (per_owner, per_owner), 1)
    ).astype(f32).astype(bf16)

    def ranks(o):
        cell_of = idx_ref[o, 0:1, :]
        marks = cell_of == lax.broadcasted_iota(jnp.int32, (cells, per_owner), 0).astype(f32)
        marks = jnp.where(marks, 1.0, 0.0)
        before = jnp.dot(marks.astype(bf16), earlier, preferred_element_type=f32)
        return cell_of, jnp.sum(marks * before, axis=0, keepdims=True)

    def index_owner(o, carry):
        cell_of, rank = ranks(o)
        place = jnp.where(cell_of == cell.astype(f32), rank, -1.0)

        def index_chunk(i, inner):
            slot = (lax.broadcasted_iota(jnp.int32, (chunk, per_owner), 0) + i * chunk) >> 3
            pick = jnp.where(place == slot.astype(f32), 1.0, 0.0)
            at = pl.ds(pl.multiple_of(i * chunk, chunk), chunk)
            for v in range(3):
                value = jnp.sum(pick * idx_ref[o, v + 1 : v + 2, :], axis=1, keepdims=True)
                slots[o, v, at] = jnp.broadcast_to(value, (chunk, 128))
            return inner

        lax.fori_loop(0, held_rows // chunk, index_chunk, 0)
        return carry

    lax.fori_loop(0, owners, index_owner, 0)
    apart = jnp.abs(r - c)
    for s in range(1, n):
        for h in range(HALVES):
            for side in range(2):
                k, there = from_side(side, s)

                @pl.when(there)
                def _():
                    l_copy(k, h, side, False).wait_recv()

                    @pl.when(can(side))
                    def _():
                        l_copy(k, h, side, False).start()

            for side in range(2):
                k, there = from_side(side, s)

                @pl.when(there)
                def _():
                    partial(k, h, False)

        if s + 1 < n:
            lx_copy(s + 1).start()
        if s >= 2:
            @pl.when(apart == s - 2)
            def _():
                finish()

    @pl.when(apart >= n - 2)
    def _():
        finish()

    for j in range(1, n):
        lx_wait(j)
    for t in range(1, n):
        for h in range(HALVES):
            for side in range(2):
                k, there = from_side(side, t)

                @pl.when(there)
                def _():
                    c_copy(k, h, side).wait_recv()

                    @pl.when(can(side))
                    def _():
                        c_copy(k, h, side).start()

        if t == 1:
            accumulate(c, True)
        else:
            for side in range(2):
                k, there = from_side(side, t - 1)

                @pl.when(there)
                def _():
                    accumulate(k, False)

    for side in range(2):
        k, there = from_side(side, n - 1)

        @pl.when(there)
        def _():
            accumulate(k, False)

    def write(i, carry):
        at = pl.ds(pl.multiple_of(i * step, step), step)
        block_ref[at] = (inv_ref[at].astype(f32) - prod_ref[at]).astype(bf16)
        return carry

    lax.fori_loop(0, size // step, write, 0)

    lanes = 2 * B * B
    part_lanes = B * B

    def spread(total, transposed):
        at = lax.broadcasted_iota(jnp.int32, (2 * total, lanes), 0)
        to = lax.broadcasted_iota(jnp.int32, (2 * total, lanes), 1)
        half_of = (at >= total) == (to >= part_lanes)
        inner = ((to & (part_lanes - 1)) >> 3) if transposed else (to & 7)
        return jnp.where(half_of & ((at & 7) == inner), 1.0, 0.0).astype(bf16)

    spread_super = spread(size, False)
    spread_trail = spread(width, True)
    lane = lax.broadcasted_iota(jnp.int32, (chunk, lanes), 1)
    inside = lax.broadcasted_iota(jnp.int32, (chunk, lanes), 0) & 7
    keep_super = ((lane & (part_lanes - 1)) >> 3) == inside
    keep_trail = (lane & 7) == inside
    group = jnp.where(
        lax.broadcasted_iota(jnp.int32, (chunk // B, chunk), 0)
        == (lax.broadcasted_iota(jnp.int32, (chunk // B, chunk), 1) >> 3),
        1.0,
        0.0,
    ).astype(bf16)
    row_of = lax.broadcasted_iota(jnp.int32, (chunk, size), 1).astype(f32)
    row_in = (lax.broadcasted_iota(jnp.int32, (chunk, 1), 0) & 7).astype(f32)
    col_super = lax.broadcasted_iota(jnp.int32, (chunk, 2 * size), 1)
    col_super = jnp.where(col_super >= size, col_super - size, col_super).astype(f32)
    col_trail = lax.broadcasted_iota(jnp.int32, (chunk, 2 * width), 1)
    col_trail = jnp.where(col_trail >= width, col_trail - width, col_trail).astype(f32)
    last = float(B - 1)

    def gather_owner(o, carry):
        def gather_chunk(i, inner):
            at = pl.ds(pl.multiple_of(i * chunk, chunk), chunk)
            first_row = slots[o, 0, at][:, :1]
            first_super = slots[o, 1, at][:, :1]
            first_trail = slots[o, 2, at][:, :1]
            pick = jnp.where(row_of == first_row + row_in, 1.0, 0.0).astype(bf16)
            taken = jnp.dot(pick, block_ref[...], preferred_element_type=f32)
            taken = jnp.where(
                (col_super >= first_super) & (col_super <= first_super + last), taken, 0.0
            ).astype(bf16)
            out_super = jnp.dot(taken, spread_super, preferred_element_type=f32)
            taken = jnp.dot(pick, cz[c], preferred_element_type=f32)
            taken = jnp.where(
                (col_trail >= first_trail) & (col_trail <= first_trail + last), taken, 0.0
            ).astype(bf16)
            out_trail = jnp.dot(taken, spread_trail, preferred_element_type=f32)
            both = jnp.where(keep_super, out_super, 0.0) + jnp.where(keep_trail, out_trail, 0.0)
            value = jnp.dot(group, both.astype(bf16), preferred_element_type=f32)
            swapped = jnp.concatenate([value[:, part_lanes:], value[:, :part_lanes]], axis=1)
            to = pl.ds(pl.multiple_of(i * (chunk // B), chunk // B), chunk // B)
            term[o, to] = weight_ref[0:1] * value + weight_ref[1:2] * swapped
            return inner

        lax.fori_loop(0, held_rows // chunk, gather_chunk, 0)
        return carry

    lax.fori_loop(0, owners, gather_owner, 0)

    def term_copy(j):
        to = lax.rem(me + j, owners)
        return pltpu.make_async_remote_copy(
            src_ref=term.at[to], dst_ref=pool.at[j], send_sem=term_send.at[j],
            recv_sem=term_recv.at[j], device_id={"pole": to}, device_id_type=MESH,
        )

    for j in range(1, owners):
        term_copy(j).start()
    for j in range(1, owners):
        term_copy(j).wait_recv()
    total = term[me]
    for j in range(1, owners):
        total = total + pool[j]
    coll[cell] = total

    def coll_copy(j):
        return pltpu.make_async_remote_copy(
            src_ref=coll.at[cell], dst_ref=coll.at[cell], send_sem=coll_send.at[j],
            recv_sem=coll_recv.at[cell], device_id=peer(j)[0], device_id_type=MESH,
        )

    def coll_wait(j):
        where, other = peer(j)
        pltpu.make_async_remote_copy(
            src_ref=coll.at[other], dst_ref=coll.at[other], send_sem=coll_send.at[j],
            recv_sem=coll_recv.at[other], device_id=where, device_id_type=MESH,
        ).wait_recv()

    for j in range(1, cells):
        coll_copy(j).start()
    cell_of, rank = ranks(me)
    target = jnp.broadcast_to(cell_of * most + rank, (128, per_owner))
    target = jnp.transpose(target)
    for j in range(1, cells):
        coll_wait(j)
    for q in range(per_owner // 128):
        mine = target[q * 128 : (q + 1) * 128, :1]
        pick = jnp.where(
            mine == lax.broadcasted_iota(jnp.int32, (128, cells * most), 1).astype(f32), 1.0, 0.0
        ).astype(bf16)
        rest = coll[...].reshape(cells * most, lanes)
        summed = jnp.zeros((128, lanes), f32)
        for _ in range(3):
            top = rest.astype(bf16)
            rest = rest - top.astype(f32)
            summed = summed + jnp.dot(pick, top, preferred_element_type=f32)
        dens_ref[q * 128 : (q + 1) * 128] = summed * proj_ref[q * 128 : (q + 1) * 128]

    for j in range(1, owners):
        term_copy(j).wait_send()
    for j in range(1, cells):
        coll_copy(j).wait_send()
    for j in range(1, n):
        lx_copy(j).wait_send()
        for h in range(HALVES):
            rs_copy(lax.rem(r + j, n), h).wait_send()
    for s in range(n):
        for h in range(HALVES):
            for side in range(2):
                k, there = from_side(side, s)

                @pl.when(there & can(side))
                def _():
                    l_copy(k, h, side, s == 0).wait_send()
                    c_copy(k, h, side).wait_send()


def products(n, owners, lower, trail, inverse, idx, weight, projector):
    size = lower.shape[0]
    wide = lower.shape[1]
    bf16 = jnp.bfloat16
    lanes = 2 * B * B
    most = 2 * idx.shape[2] // (n * n)
    dma = pltpu.SemaphoreType.DMA
    vmem = pl.BlockSpec(memory_space=pltpu.VMEM)
    return pl.pallas_call(
        functools.partial(main_kernel, n),
        name="products",
        out_shape=(
            jax.ShapeDtypeStruct((size, 2 * size), bf16),
            jax.ShapeDtypeStruct(projector.shape, jnp.float32),
        ),
        in_specs=[vmem] * 6,
        out_specs=(vmem, vmem),
        scratch_shapes=[
            pltpu.VMEM((owners, most, lanes), jnp.float32),
            pltpu.VMEM((owners, most, lanes), jnp.float32),
            pltpu.VMEM((n * n, most, lanes), jnp.float32),
            pltpu.VMEM((owners, 3, most * B, 128), jnp.float32),
            dma((owners,)),
            dma((owners,)),
            dma((n * n,)),
            dma((n * n,)),
            pltpu.VMEM((size, 2 * size), jnp.float32),
            pltpu.VMEM((n, size, wide), bf16),
            pltpu.VMEM((n, size, wide), bf16),
            pltpu.VMEM((n, size, wide), bf16),
            pltpu.VMEM((size, wide), jnp.float32),
            pltpu.VMEM((n, size, wide), bf16),
            pltpu.VMEM((n, size, wide), bf16),
            pltpu.VMEM((wide, wide), bf16),
            dma((2, n, HALVES)),
            dma((n, HALVES)),
            dma((n,)),
            dma((n,)),
            dma((n, HALVES)),
            dma((n, HALVES)),
            dma((2, n, HALVES)),
            dma((n, HALVES)),
        ],
        compiler_params=pltpu.CompilerParams(
            collective_id=0, has_side_effects=True, vmem_limit_bytes=40 * 1024 * 1024
        ),
    )(lower, trail, inverse, idx, weight, projector)


def local(
    inverse_trail, lower_t, diag_inverse, pole_weight, pole_slot, pair_row, pair_col, projector
):
    trail = inverse_trail[0]
    lower = lower_t[0]
    inverse = diag_inverse[0]
    n = lax.axis_size("row")
    owners = lax.axis_size("pole")
    f32 = jnp.float32
    size = lower.shape[0]
    atoms = size // B
    trail_atoms = trail.shape[2] // B
    in_super = pair_row < atoms * n
    trail_atom = jnp.maximum(pair_row - atoms * n, 0)
    row_atom = jnp.where(in_super, pair_row, pair_col)
    col_atom = jnp.where(in_super, pair_col, trail_atom)
    cell_row = row_atom // atoms
    cell_col = jnp.where(in_super, col_atom // atoms, col_atom // trail_atoms)
    away = -8 * size
    row_first = (row_atom - cell_row * atoms) * B
    super_first = jnp.where(in_super, (col_atom - cell_col * atoms) * B, away)
    trail_first = jnp.where(in_super, away, (col_atom - cell_col * trail_atoms) * B)
    idx = jnp.stack(
        [
            x.reshape(owners, -1).astype(f32)
            for x in (cell_row * n + cell_col, row_first, super_first, trail_first)
        ],
        axis=1,
    )
    selector = (jnp.arange(pole_weight.shape[0], dtype=jnp.int32) == pole_slot[0]).astype(f32)
    weight = jnp.sum(selector[:, None] * pole_weight, axis=0)
    sign = jnp.where(jnp.arange(2 * B * B) < B * B, -1.0, 1.0).astype(f32)
    weight = jnp.stack([jnp.full((2 * B * B,), weight[0]), sign * weight[1]])
    projector = projector.astype(f32)
    projector = jnp.concatenate([projector, projector], axis=1)
    block, density = products(
        n,
        owners,
        lower.reshape(size, -1),
        trail.reshape(trail.shape[0], -1),
        inverse.reshape(size, -1),
        idx,
        weight,
        projector,
    )
    return block.reshape(1, size, 2, size), density


def solution(mesh):
    in_specs = (
        P("pole", "row", None, "col"),
        P("pole", "col", None, "row"),
        P("pole", "row", None, "col"),
        P(),
        P("pole"),
        P(),
        P(),
        P("pole", None),
    )
    out_specs = (P("pole", "row", None, "col"), P("pole", None))
    return jax.shard_map(local, mesh=mesh, in_specs=in_specs, out_specs=out_specs, check_vma=False)
```

time: 319 us -> 129 us (0.40)
  the two profiles are of different devices: /device:TPU:0 before, /device:TPU:28 now
where the time goes in v1:
time: 129 us; the launch traced here: 128 us
  Pallas kernels  119 us (92%)
  local copies, waits for them, and re-layouts  5.05 us (4%)
  other arithmetic  2.31 us (2%)
  between operations  1.42 us (1%)
    pallas_call x1, Pallas kernels, products(): pl.pallas_call(functools.partial(main_kernel, n), name='products', out_sh...  119 us

profile of v1, /device:TPU:28, one launch (start us, length us, event | category | flops | bytes accessed | tf_op | source)
XLA Modules:
  0.0 128.0 jit_solution(16675457017581797888)
XLA Ops:
  0.6 0.0 copy-start.3
  1.3 0.8 multiply_reduce_fusion
  2.1 0.6 fusion.7
  2.7 0.6 fusion.6
  3.4 0.7 stack.5.weight_ref
  4.0 0.7 add_convert_fusion
  4.8 0.0 copy-start.2
  4.8 0.0 copy-start.1
  4.8 0.0 copy-done.3
  4.8 0.0 copy-start
  4.8 0.1 copy.10
  5.0 0.1 maximum_convert_fusion.proj_ref
  5.1 0.6 copy-done.2
  5.7 0.1 copy-done.1
  5.9 0.1 copy.12
  6.0 0.3 copy-done
  6.2 0.2 copy.14
  6.5 119.2 %products.1 = (bf16[512,1024]{1,0:T(8,128)(2,1)S(1)}, f32[512,128]{1,0:T(8,128)S(1)}) custom-call(bf16[512,512]{1,0:T(8,128)(2,1)S(1)} %bitcast.18, bf16[256,512]{1,0:T(8,128)(2,1)S(1)} %bitcast.19, bf16[512,1024]{1,0:T(8,128)(2,1)S(1)} %bitcast.17, f32[2,4,512]{2,1,0:T(4,128)S(1)} %pad_maximum_fusion.idx_ref, f32[2,128]{1,0:T(2,128)S(1)} %stack.5.weight_ref, ...), custom_call_target="tpu_custom_call" | custom-call | tf_op jit(solution)/shard_map/products/pallas_call | solution.py:437
  125.7 1.6 %reshape.73 = bf16[1,512,2,512]{3,2,1,0:T(2,128)(2,1)} reshape(bf16[512,1024]{1,0:T(8,128)(2,1)S(1)} %get-tuple-element.4) | data formatting | bytes 2097152 | tf_op jit(solution)/shard_map/reshape | solution.py:523
  127.3 0.7 copy.17
  (3 shorter events, 0.1 us)
Async XLA Ops:
  0.6 4.2 %copy-start.3 = (bf16[512,64]{0,1:T(8,128)(2,1)S(1)}, bf16[512,64]{0,1:T(8,128)(2,1)}, u32[]{:S(2)}) copy-start(bf16[512,64]{0,1:T(8,128)(2,1)} %param.15) | copy-start | bytes 196612
  4.8 1.0 copy-start.2
  4.8 1.1 copy-start.1
  4.8 1.4 %copy-start = (bf16[1,512,2,512]{3,2,1,0:T(2,128)(2,1)S(1)}, bf16[1,512,2,512]{3,2,1,0:T(2,128)(2,1)}, u32[]{:S(2)}) copy-start(bf16[1,512,2,512]{3,2,1,0:T(2,128)(2,1)} %param.10) | copy-start | bytes 3145732

commit v2 on v1

--- a/solution.py
+++ b/solution.py
@@ -8,7 +8,7 @@
 from jax.sharding import PartitionSpec as P
 
 B = 8
-HALVES = 2
+HALVES = 4
 MESH = pl.DeviceIdType.MESH
 
 
@@ -33,15 +33,12 @@
     cells = n * n
     cell = r * n + c
 
-    def peer(j):
-        other = lax.rem(cell + j, cells)
-        return {"row": other // n, "col": lax.rem(other, n)}, other
-
-    for j in range(1, cells):
-        pl.semaphore_signal(barrier, inc=1, device_id=peer(j)[0], device_id_type=MESH)
+    for j in range(1, n):
+        pl.semaphore_signal(barrier, inc=1, device_id={"row": lax.rem(r + j, n)}, device_id_type=MESH)
+        pl.semaphore_signal(barrier, inc=1, device_id={"col": lax.rem(c + j, n)}, device_id_type=MESH)
     for j in range(1, owners):
         pl.semaphore_signal(barrier, inc=1, device_id={"pole": lax.rem(me + j, owners)}, device_id_type=MESH)
-    pl.semaphore_wait(barrier, cells - 1 + owners - 1)
+    pl.semaphore_wait(barrier, 2 * (n - 1) + owners - 1)
 
     def rows(h):
         return pl.ds(h * half, half)
@@ -193,7 +190,8 @@
     treal[width:, width:] = trail_re
     for h in range(HALVES):
         partial(c, h, True)
-    lx_copy(1).start()
+    for j in range(1, n):
+        lx_copy(j).start()
 
     per_owner = idx_ref.shape[2]
     most = 2 * per_owner // cells
@@ -249,8 +247,6 @@
                 def _():
                     partial(k, h, False)
 
-        if s + 1 < n:
-            lx_copy(s + 1).start()
         if s >= 2:
             @pl.when(apart == s - 2)
             def _():
@@ -374,26 +370,31 @@
         total = total + pool[j]
     coll[cell] = total
 
-    def coll_copy(j):
+    def coll_copy(j, at_col):
+        at = r * n + at_col
         return pltpu.make_async_remote_copy(
-            src_ref=coll.at[cell], dst_ref=coll.at[cell], send_sem=coll_send.at[j],
-            recv_sem=coll_recv.at[cell], device_id=peer(j)[0], device_id_type=MESH,
+            src_ref=coll.at[at], dst_ref=coll.at[at], send_sem=coll_send.at[j],
+            recv_sem=coll_recv.at[at_col], device_id={"col": lax.rem(c + j, n)}, device_id_type=MESH,
         )
 
-    def coll_wait(j):
-        where, other = peer(j)
-        pltpu.make_async_remote_copy(
-            src_ref=coll.at[other], dst_ref=coll.at[other], send_sem=coll_send.at[j],
-            recv_sem=coll_recv.at[other], device_id=where, device_id_type=MESH,
-        ).wait_recv()
-
-    for j in range(1, cells):
-        coll_copy(j).start()
+    def group_copy(j, at_row):
+        at = pl.ds(at_row * n, n)
+        return pltpu.make_async_remote_copy(
+            src_ref=coll.at[at], dst_ref=coll.at[at], send_sem=coll_send.at[n + j],
+            recv_sem=coll_recv.at[n + at_row], device_id={"row": lax.rem(r + j, n)}, device_id_type=MESH,
+        )
+
+    for j in range(1, n):
+        coll_copy(j, c).start()
     cell_of, rank = ranks(me)
     target = jnp.broadcast_to(cell_of * most + rank, (128, per_owner))
     target = jnp.transpose(target)
-    for j in range(1, cells):
-        coll_wait(j)
+    for j in range(1, n):
+        coll_copy(j, lax.rem(c + j, n)).wait_recv()
+    for j in range(1, n):
+        group_copy(j, r).start()
+    for j in range(1, n):
+        group_copy(j, lax.rem(r + j, n)).wait_recv()
     for q in range(per_owner // 128):
         mine = target[q * 128 : (q + 1) * 128, :1]
         pick = jnp.where(
@@ -409,8 +410,9 @@
 
     for j in range(1, owners):
         term_copy(j).wait_send()
-    for j in range(1, cells):
-        coll_copy(j).wait_send()
+    for j in range(1, n):
+        coll_copy(j, c).wait_send()
+        group_copy(j, r).wait_send()
     for j in range(1, n):
         lx_copy(j).wait_send()
         for h in range(HALVES):
@@ -450,8 +452,8 @@
             pltpu.VMEM((owners, 3, most * B, 128), jnp.float32),
             dma((owners,)),
             dma((owners,)),
-            dma((n * n,)),
-            dma((n * n,)),
+            dma((2 * n,)),
+            dma((2 * n,)),
             pltpu.VMEM((size, 2 * size), jnp.float32),
             pltpu.VMEM((n, size, wide), bf16),
             pltpu.VMEM((n, size, wide), bf16),

time: 129 us -> 116 us (0.90)
  Pallas kernels: 119 us -> 107 us
    pallas_call x1, Pallas kernels: 119 us -> 107 us  [products(): pl.pallas_call(functools.partial(main_kernel, n), name='products', out_sh...]
where the time goes in v2:
time: 116 us
  Pallas kernels  107 us (92%)
  local copies, waits for them, and re-layouts  5.05 us (4%)
  other arithmetic  2.31 us (2%)
  between operations  1.42 us (1%)
    pallas_call x1, Pallas kernels, products(): pl.pallas_call(functools.partial(main_kernel, n), name='products', out_sh...  107 us

profile of v2, /device:TPU:28, one launch (start us, length us, event | category | flops | bytes accessed | tf_op | source)
XLA Modules:
  0.0 115.9 jit_solution(6303318916725027437)
XLA Ops:
  0.6 0.0 copy-start.3
  1.3 0.8 multiply_reduce_fusion
  2.1 0.6 fusion.7
  2.7 0.6 fusion.6
  3.4 0.7 stack.5.weight_ref
  4.0 0.7 add_convert_fusion
  4.8 0.0 copy-start.2
  4.8 0.0 copy-start.1
  4.8 0.0 copy-done.3
  4.8 0.0 copy-start
  4.8 0.1 copy.10
  5.0 0.1 maximum_convert_fusion.proj_ref
  5.1 0.6 copy-done.2
  5.7 0.1 copy-done.1
  5.9 0.1 copy.12
  6.0 0.3 copy-done
  6.2 0.2 copy.14
  6.5 107.1 %products.1 = (bf16[512,1024]{1,0:T(8,128)(2,1)S(1)}, f32[512,128]{1,0:T(8,128)S(1)}) custom-call(bf16[512,512]{1,0:T(8,128)(2,1)S(1)} %bitcast.18, bf16[256,512]{1,0:T(8,128)(2,1)S(1)} %bitcast.19, bf16[512,1024]{1,0:T(8,128)(2,1)S(1)} %bitcast.17, f32[2,4,512]{2,1,0:T(4,128)S(1)} %pad_maximum_fusion.idx_ref, f32[2,128]{1,0:T(2,128)S(1)} %stack.5.weight_ref, ...), custom_call_target="tpu_custom_call" | custom-call | tf_op jit(solution)/shard_map/products/pallas_call | solution.py:439
  113.6 1.6 %reshape.73 = bf16[1,512,2,512]{3,2,1,0:T(2,128)(2,1)} reshape(bf16[512,1024]{1,0:T(8,128)(2,1)S(1)} %get-tuple-element.4) | data formatting | bytes 2097152 | tf_op jit(solution)/shard_map/reshape | solution.py:525
  115.2 0.7 copy.17
  (3 shorter events, 0.1 us)
Async XLA Ops:
  0.6 4.2 %copy-start.3 = (bf16[512,64]{0,1:T(8,128)(2,1)S(1)}, bf16[512,64]{0,1:T(8,128)(2,1)}, u32[]{:S(2)}) copy-start(bf16[512,64]{0,1:T(8,128)(2,1)} %param.15) | copy-start | bytes 196612
  4.8 1.0 copy-start.2
  4.8 1.1 copy-start.1
  4.8 1.4 %copy-start = (bf16[1,512,2,512]{3,2,1,0:T(2,128)(2,1)S(1)}, bf16[1,512,2,512]{3,2,1,0:T(2,128)(2,1)}, u32[]{:S(2)}) copy-start(bf16[1,512,2,512]{3,2,1,0:T(2,128)(2,1)} %param.10) | copy-start | bytes 3145732

commit v3 on v2

--- a/solution.py
+++ b/solution.py
@@ -13,8 +13,8 @@
 
 
 def main_kernel(
-    n, l_ref, t_ref, inv_ref, idx_ref, weight_ref, proj_ref, block_ref, dens_ref,
-    term, pool, coll, slots, term_send, term_recv, coll_send, coll_recv, prod_ref,
+    n, l_ref, t_ref, inv_ref, prow_ref, pcol_ref, table_ref, slot_ref, proj_ref, block_ref, dens_ref,
+    idx_ref, weight_ref, term, pool, coll, slots, term_send, term_recv, coll_send, coll_recv, prod_ref,
     lz, lx, part, own, rs, cz, treal,
     lz_send, lz_recv, lx_send, lx_recv, rs_send, rs_recv, cz_send, cz_recv,
 ):
@@ -193,6 +193,31 @@
     for j in range(1, n):
         lx_copy(j).start()
 
+    atoms = size // B
+    trail_atoms = width // B
+
+    def split(value, by):
+        whole = jnp.floor((value + 0.5) * (1.0 / by))
+        return whole, value - whole * by
+
+    pair_row = prow_ref[...].astype(f32)
+    pair_col = pcol_ref[...].astype(f32)
+    in_super = pair_row < float(atoms * n)
+    trail_atom = jnp.maximum(pair_row - float(atoms * n), 0.0)
+    cell_row, row_in_cell = split(jnp.where(in_super, pair_row, pair_col), atoms)
+    col_super, super_in_cell = split(pair_col, atoms)
+    col_trail, trail_in_cell = split(trail_atom, trail_atoms)
+    away = float(-8 * size)
+    idx_ref[:, 0] = cell_row * n + jnp.where(in_super, col_super, col_trail)
+    idx_ref[:, 1] = row_in_cell * B
+    idx_ref[:, 2] = jnp.where(in_super, super_in_cell * B, away)
+    idx_ref[:, 3] = jnp.where(in_super, away, trail_in_cell * B)
+    table = table_ref[...]
+    chosen = lax.broadcasted_iota(jnp.int32, table.shape, 0) == slot_ref[0]
+    chosen = jnp.sum(jnp.where(chosen, table, 0.0), axis=0, keepdims=True)
+    all_lanes = lax.broadcasted_iota(jnp.int32, (1, 2 * B * B), 1)
+    weight_ref[0:1] = jnp.broadcast_to(chosen[:, 0:1], (1, 2 * B * B))
+    weight_ref[1:2] = jnp.where(all_lanes < B * B, -1.0, 1.0) * chosen[:, 1:2]
     per_owner = idx_ref.shape[2]
     most = 2 * per_owner // cells
     held_rows = most * B
@@ -255,45 +280,6 @@
     @pl.when(apart >= n - 2)
     def _():
         finish()
-
-    for j in range(1, n):
-        lx_wait(j)
-    for t in range(1, n):
-        for h in range(HALVES):
-            for side in range(2):
-                k, there = from_side(side, t)
-
-                @pl.when(there)
-                def _():
-                    c_copy(k, h, side).wait_recv()
-
-                    @pl.when(can(side))
-                    def _():
-                        c_copy(k, h, side).start()
-
-        if t == 1:
-            accumulate(c, True)
-        else:
-            for side in range(2):
-                k, there = from_side(side, t - 1)
-
-                @pl.when(there)
-                def _():
-                    accumulate(k, False)
-
-    for side in range(2):
-        k, there = from_side(side, n - 1)
-
-        @pl.when(there)
-        def _():
-            accumulate(k, False)
-
-    def write(i, carry):
-        at = pl.ds(pl.multiple_of(i * step, step), step)
-        block_ref[at] = (inv_ref[at].astype(f32) - prod_ref[at]).astype(bf16)
-        return carry
-
-    lax.fori_loop(0, size // step, write, 0)
 
     lanes = 2 * B * B
     part_lanes = B * B
@@ -325,24 +311,75 @@
     col_trail = jnp.where(col_trail >= width, col_trail - width, col_trail).astype(f32)
     last = float(B - 1)
 
+    def trail_owner(o, carry):
+        def trail_chunk(i, inner):
+            at = pl.ds(pl.multiple_of(i * chunk, chunk), chunk)
+            first_row = slots[o, 0, at][:, :1]
+            first_trail = slots[o, 2, at][:, :1]
+            pick = jnp.where(row_of == first_row + row_in, 1.0, 0.0).astype(bf16)
+            taken = jnp.dot(pick, cz[c], preferred_element_type=f32)
+            taken = jnp.where(
+                (col_trail >= first_trail) & (col_trail <= first_trail + last), taken, 0.0
+            ).astype(bf16)
+            out_trail = jnp.dot(taken, spread_trail, preferred_element_type=f32)
+            slots[o, 2, at] = jnp.where(keep_trail, out_trail, 0.0)
+            return inner
+
+        lax.fori_loop(0, held_rows // chunk, trail_chunk, 0)
+        return carry
+
+    for j in range(1, n):
+        lx_wait(j)
+    for t in range(1, n):
+        for h in range(HALVES):
+            for side in range(2):
+                k, there = from_side(side, t)
+
+                @pl.when(there)
+                def _():
+                    c_copy(k, h, side).wait_recv()
+
+                    @pl.when(can(side))
+                    def _():
+                        c_copy(k, h, side).start()
+
+        if t == 1:
+            accumulate(c, True)
+            lax.fori_loop(0, owners, trail_owner, 0)
+        else:
+            for side in range(2):
+                k, there = from_side(side, t - 1)
+
+                @pl.when(there)
+                def _():
+                    accumulate(k, False)
+
+    for side in range(2):
+        k, there = from_side(side, n - 1)
+
+        @pl.when(there)
+        def _():
+            accumulate(k, False)
+
+    def write(i, carry):
+        at = pl.ds(pl.multiple_of(i * step, step), step)
+        block_ref[at] = (inv_ref[at].astype(f32) - prod_ref[at]).astype(bf16)
+        return carry
+
+    lax.fori_loop(0, size // step, write, 0)
+
     def gather_owner(o, carry):
         def gather_chunk(i, inner):
             at = pl.ds(pl.multiple_of(i * chunk, chunk), chunk)
             first_row = slots[o, 0, at][:, :1]
             first_super = slots[o, 1, at][:, :1]
-            first_trail = slots[o, 2, at][:, :1]
             pick = jnp.where(row_of == first_row + row_in, 1.0, 0.0).astype(bf16)
             taken = jnp.dot(pick, block_ref[...], preferred_element_type=f32)
             taken = jnp.where(
                 (col_super >= first_super) & (col_super <= first_super + last), taken, 0.0
             ).astype(bf16)
             out_super = jnp.dot(taken, spread_super, preferred_element_type=f32)
-            taken = jnp.dot(pick, cz[c], preferred_element_type=f32)
-            taken = jnp.where(
-                (col_trail >= first_trail) & (col_trail <= first_trail + last), taken, 0.0
-            ).astype(bf16)
-            out_trail = jnp.dot(taken, spread_trail, preferred_element_type=f32)
-            both = jnp.where(keep_super, out_super, 0.0) + jnp.where(keep_trail, out_trail, 0.0)
+            both = jnp.where(keep_super, out_super, 0.0) + slots[o, 2, at]
             value = jnp.dot(group, both.astype(bf16), preferred_element_type=f32)
             swapped = jnp.concatenate([value[:, part_lanes:], value[:, :part_lanes]], axis=1)
             to = pl.ds(pl.multiple_of(i * (chunk // B), chunk // B), chunk // B)
@@ -351,8 +388,6 @@
 
         lax.fori_loop(0, held_rows // chunk, gather_chunk, 0)
         return carry
-
-    lax.fori_loop(0, owners, gather_owner, 0)
 
     def term_copy(j):
         to = lax.rem(me + j, owners)
@@ -362,7 +397,9 @@
         )
 
     for j in range(1, owners):
+        gather_owner(lax.rem(me + j, owners), 0)
         term_copy(j).start()
+    gather_owner(me, 0)
     for j in range(1, owners):
         term_copy(j).wait_recv()
     total = term[me]
@@ -406,7 +443,8 @@
             top = rest.astype(bf16)
             rest = rest - top.astype(f32)
             summed = summed + jnp.dot(pick, top, preferred_element_type=f32)
-        dens_ref[q * 128 : (q + 1) * 128] = summed * proj_ref[q * 128 : (q + 1) * 128]
+        mine = proj_ref[q * 128 : (q + 1) * 128].astype(f32)
+        dens_ref[q * 128 : (q + 1) * 128] = summed * jnp.concatenate([mine, mine], axis=1)
 
     for j in range(1, owners):
         term_copy(j).wait_send()
@@ -428,12 +466,13 @@
                     c_copy(k, h, side).wait_send()
 
 
-def products(n, owners, lower, trail, inverse, idx, weight, projector):
+def products(n, owners, lower, trail, inverse, pair_row, pair_col, table, slot, projector):
     size = lower.shape[0]
     wide = lower.shape[1]
     bf16 = jnp.bfloat16
     lanes = 2 * B * B
-    most = 2 * idx.shape[2] // (n * n)
+    per_owner = projector.shape[0]
+    most = 2 * per_owner // (n * n)
     dma = pltpu.SemaphoreType.DMA
     vmem = pl.BlockSpec(memory_space=pltpu.VMEM)
     return pl.pallas_call(
@@ -441,11 +480,13 @@
         name="products",
         out_shape=(
             jax.ShapeDtypeStruct((size, 2 * size), bf16),
-            jax.ShapeDtypeStruct(projector.shape, jnp.float32),
+            jax.ShapeDtypeStruct((per_owner, lanes), jnp.float32),
         ),
-        in_specs=[vmem] * 6,
+        in_specs=[vmem] * 6 + [pl.BlockSpec(memory_space=pltpu.SMEM), vmem],
         out_specs=(vmem, vmem),
         scratch_shapes=[
+            pltpu.VMEM((owners, 4, per_owner), jnp.float32),
+            pltpu.VMEM((2, lanes), jnp.float32),
             pltpu.VMEM((owners, most, lanes), jnp.float32),
             pltpu.VMEM((owners, most, lanes), jnp.float32),
             pltpu.VMEM((n * n, most, lanes), jnp.float32),
@@ -474,7 +515,7 @@
         compiler_params=pltpu.CompilerParams(
             collective_id=0, has_side_effects=True, vmem_limit_bytes=40 * 1024 * 1024
         ),
-    )(lower, trail, inverse, idx, weight, projector)
+    )(lower, trail, inverse, pair_row, pair_col, table, slot, projector)
 
 
 def local(
@@ -485,41 +526,17 @@
     inverse = diag_inverse[0]
     n = lax.axis_size("row")
     owners = lax.axis_size("pole")
-    f32 = jnp.float32
     size = lower.shape[0]
-    atoms = size // B
-    trail_atoms = trail.shape[2] // B
-    in_super = pair_row < atoms * n
-    trail_atom = jnp.maximum(pair_row - atoms * n, 0)
-    row_atom = jnp.where(in_super, pair_row, pair_col)
-    col_atom = jnp.where(in_super, pair_col, trail_atom)
-    cell_row = row_atom // atoms
-    cell_col = jnp.where(in_super, col_atom // atoms, col_atom // trail_atoms)
-    away = -8 * size
-    row_first = (row_atom - cell_row * atoms) * B
-    super_first = jnp.where(in_super, (col_atom - cell_col * atoms) * B, away)
-    trail_first = jnp.where(in_super, away, (col_atom - cell_col * trail_atoms) * B)
-    idx = jnp.stack(
-        [
-            x.reshape(owners, -1).astype(f32)
-            for x in (cell_row * n + cell_col, row_first, super_first, trail_first)
-        ],
-        axis=1,
-    )
-    selector = (jnp.arange(pole_weight.shape[0], dtype=jnp.int32) == pole_slot[0]).astype(f32)
-    weight = jnp.sum(selector[:, None] * pole_weight, axis=0)
-    sign = jnp.where(jnp.arange(2 * B * B) < B * B, -1.0, 1.0).astype(f32)
-    weight = jnp.stack([jnp.full((2 * B * B,), weight[0]), sign * weight[1]])
-    projector = projector.astype(f32)
-    projector = jnp.concatenate([projector, projector], axis=1)
     block, density = products(
         n,
         owners,
         lower.reshape(size, -1),
         trail.reshape(trail.shape[0], -1),
         inverse.reshape(size, -1),
-        idx,
-        weight,
+        pair_row.reshape(owners, -1),
+        pair_col.reshape(owners, -1),
+        pole_weight,
+        pole_slot,
         projector,
     )
     return block.reshape(1, size, 2, size), density

time: 116 us -> 112 us (0.966)
  Pallas kernels: 107 us -> 103 us
  other arithmetic: 2.31 us -> 0 us
  local copies, waits for them, and re-layouts: 5.05 us -> 7.12 us
    pallas_call x1, Pallas kernels: 107 us -> 103 us  [products(): pl.pallas_call(functools.partial(main_kernel, n), name='products', out_sh...]
    unnamed x13 -> x10, local copies, waits for them, and re-layouts: 2.23 us -> 4.83 us
where the time goes in v3:
time: 112 us; the launch traced here: 111 us
  Pallas kernels  103 us (92%)
  local copies, waits for them, and re-layouts  7.12 us (6%)
  between operations  1.44 us (1%)
    pallas_call x1, Pallas kernels, products(): pl.pallas_call(functools.partial(main_kernel, n), name='products', out_sh...  103 us
    unnamed x10, local copies, waits for them, and re-layouts  4.83 us

profile of v3, /device:TPU:28, one launch (start us, length us, event | category | flops | bytes accessed | tf_op | source)
XLA Modules:
  0.0 111.2 jit_solution(4252122924619047668)
XLA Ops:
  0.6 0.0 copy-start.1
  0.6 0.0 copy-start
  1.4 0.0 copy-done.1
  1.4 0.7 reshape.14.pcol_ref
  2.1 0.8 copy.10.table_ref
  2.9 1.0 copy.11.proj_ref
  3.9 1.0 copy.13
  4.9 1.1 %copy.12 = bf16[64,8,2,256]{3,1,2,0:T(8,128)(2,1)S(1)} copy(bf16[64,8,2,256]{3,2,1,0:T(2,128)(2,1)} %bitcast.13) | data formatting | bytes 1048576
  6.0 0.0 copy-done
  6.0 0.2 copy.14
  6.3 102.6 %products.1 = (bf16[512,1024]{1,0:T(8,128)(2,1)S(1)}, f32[512,128]{1,0:T(8,128)S(1)}) custom-call(bf16[512,512]{1,0:T(8,128)(2,1)S(1)} %bitcast.10, bf16[256,512]{1,0:T(8,128)(2,1)S(1)} %bitcast.11, bf16[512,1024]{1,0:T(8,128)(2,1)S(1)} %bitcast.9, s32[2,512]{1,0:T(2,128)S(1)} %reshape.13.prow_ref, s32[2,512]{1,0:T(2,128)S(1)} %reshape.14.pcol_ref, ...), custom_call_target="tpu_custom_call" | custom-call | tf_op jit(solution)/shard_map/products/pallas_call | solution.py:478
  108.9 1.6 %reshape.15 = bf16[1,512,2,512]{3,2,1,0:T(2,128)(2,1)} reshape(bf16[512,1024]{1,0:T(8,128)(2,1)S(1)} %get-tuple-element.4) | data formatting | bytes 2097152 | tf_op jit(solution)/shard_map/reshape | solution.py:542
  110.5 0.7 copy.17
  (1 shorter events, 0.0 us)
Async XLA Ops:
  0.6 0.8 copy-start.1
  0.6 5.4 %copy-start = (bf16[1,512,2,512]{3,2,1,0:T(2,128)(2,1)S(1)}, bf16[1,512,2,512]{3,2,1,0:T(2,128)(2,1)}, u32[]{:S(2)}) copy-start(bf16[1,512,2,512]{3,2,1,0:T(2,128)(2,1)} %param.10) | copy-start | bytes 3145732

commit v4 on v3

--- a/solution.py
+++ b/solution.py
@@ -343,16 +343,18 @@
                     def _():
                         c_copy(k, h, side).start()
 
-        if t == 1:
-            accumulate(c, True)
-            lax.fori_loop(0, owners, trail_owner, 0)
-        else:
-            for side in range(2):
-                k, there = from_side(side, t - 1)
-
-                @pl.when(there)
-                def _():
-                    accumulate(k, False)
+            if h != min(1, HALVES - 1):
+                continue
+            if t == 1:
+                accumulate(c, True)
+                lax.fori_loop(0, owners, trail_owner, 0)
+            else:
+                for side in range(2):
+                    k, there = from_side(side, t - 1)
+
+                    @pl.when(there)
+                    def _():
+                        accumulate(k, False)
 
     for side in range(2):
         k, there = from_side(side, n - 1)

time: 112 us -> 110 us (0.982)
  Pallas kernels: 103 us -> 101 us
    pallas_call x1, Pallas kernels: 103 us -> 101 us  [products(): pl.pallas_call(functools.partial(main_kernel, n), name='products', out_sh...]
where the time goes in v4:
time: 110 us
  Pallas kernels  101 us (92%)
  local copies, waits for them, and re-layouts  7.12 us (6%)
  between operations  1.44 us (1%)
    pallas_call x1, Pallas kernels, products(): pl.pallas_call(functools.partial(main_kernel, n), name='products', out_sh...  101 us
    unnamed x10, local copies, waits for them, and re-layouts  4.83 us

profile of v4, /device:TPU:28, one launch (start us, length us, event | category | flops | bytes accessed | tf_op | source)
XLA Modules:
  0.0 109.9 jit_solution(17330053365268968717)
XLA Ops:
  0.6 0.0 copy-start.1
  0.6 0.0 copy-start
  1.4 0.0 copy-done.1
  1.4 0.7 reshape.14.pcol_ref
  2.1 0.8 copy.10.table_ref
  2.9 1.0 copy.11.proj_ref
  3.9 1.0 copy.13
  4.9 1.1 %copy.12 = bf16[64,8,2,256]{3,1,2,0:T(8,128)(2,1)S(1)} copy(bf16[64,8,2,256]{3,2,1,0:T(2,128)(2,1)} %bitcast.13) | data formatting | bytes 1048576
  6.0 0.0 copy-done
  6.0 0.2 copy.14
  6.3 101.4 %products.1 = (bf16[512,1024]{1,0:T(8,128)(2,1)S(1)}, f32[512,128]{1,0:T(8,128)S(1)}) custom-call(bf16[512,512]{1,0:T(8,128)(2,1)S(1)} %bitcast.10, bf16[256,512]{1,0:T(8,128)(2,1)S(1)} %bitcast.11, bf16[512,1024]{1,0:T(8,128)(2,1)S(1)} %bitcast.9, s32[2,512]{1,0:T(2,128)S(1)} %reshape.13.prow_ref, s32[2,512]{1,0:T(2,128)S(1)} %reshape.14.pcol_ref, ...), custom_call_target="tpu_custom_call" | custom-call | tf_op jit(solution)/shard_map/products/pallas_call | solution.py:480
  107.7 1.6 %reshape.15 = bf16[1,512,2,512]{3,2,1,0:T(2,128)(2,1)} reshape(bf16[512,1024]{1,0:T(8,128)(2,1)S(1)} %get-tuple-element.4) | data formatting | bytes 2097152 | tf_op jit(solution)/shard_map/reshape | solution.py:544
  109.2 0.7 copy.17
  (1 shorter events, 0.0 us)
Async XLA Ops:
  0.6 0.8 copy-start.1
  0.6 5.4 %copy-start = (bf16[1,512,2,512]{3,2,1,0:T(2,128)(2,1)S(1)}, bf16[1,512,2,512]{3,2,1,0:T(2,128)(2,1)}, u32[]{:S(2)}) copy-start(bf16[1,512,2,512]{3,2,1,0:T(2,128)(2,1)} %param.10) | copy-start | bytes 3145732
